TPU v7x, 32 devices: a whole 2x2x4 slice. The times are simulated.
32 devices in a mesh: tm: 4 (over y, x), res: 8 (over z, core).
Axes of the slice: x: 2, y: 2, z: 4, core: 2. Of those that a mesh axis runs over, the one named last changes fastest.
Arguments:
- node_feats: bfloat16 [4, 1024, 512], P('tm', 'res'), may hold values from -6 to 6
- edge_feats: bfloat16 [4, 1024, 60, 192], P('tm', 'res'), may hold values from -6 to 6
- node_cotan: bfloat16 [4, 1024, 512], P('tm', 'res'), may hold values from -6 to 6
- edge_cotan: bfloat16 [4, 1024, 60, 192], P('tm', 'res'), may hold values from -6 to 6
- neighbour: int32 [1024, 60], P('res'), may hold values from 0 to 383, as said below
- edge_mask: int32 [1024, 60], P('res'), may hold values from 0 to 1, as said below
- fetch_rows: int32 [8, 8, 32], P('res'), may hold values from 0 to 1023, as said below
- chain_ids: int32 [1024], P('res'), may hold values from 0 to 23, as said below
- complex_flag: int32 [1024], P('res'), may hold values from 0 to 1, as said below
- message_in: bfloat16 [1216, 512], replicated, may hold values from -0.15625 to 0.15625
- message_mid: bfloat16 [512, 512], replicated, may hold values from -0.25 to 0.25
- message_out: bfloat16 [512, 512], replicated, may hold values from -0.75 to 0.75
- gain_node: bfloat16 [512], replicated, may hold values from 0.5 to 1.5
- offset_node: bfloat16 [512], replicated, may hold values from -3 to 3
- expand_weight: bfloat16 [512, 2048], replicated, may hold values from -0.25 to 0.25
- contract_weight: bfloat16 [2048, 512], replicated, may hold values from -0.125 to 0.125
- gain_ffn: bfloat16 [512], replicated, may hold values from 0.5 to 1.5
- offset_ffn: bfloat16 [512], replicated, may hold values from -3 to 3
- update_in: bfloat16 [1216, 192], replicated, may hold values from -0.15625 to 0.15625
- update_mid: bfloat16 [192, 192], replicated, may hold values from -0.4375 to 0.4375
- update_out: bfloat16 [192, 192], replicated, may hold values from -0.4375 to 0.4375
- gain_edge: bfloat16 [192], replicated, may hold values from 0.5 to 1.5
- offset_edge: bfloat16 [192], replicated, may hold values from -3 to 3
Outputs:
- node_out: bfloat16 [4, 1024, 512], P('tm', 'res')
- edge_out: bfloat16 [4, 1024, 60, 192], P('tm', 'res')
- node_grad: float32 [4, 1024, 512], P('tm', 'res')
- edge_grad: float32 [4, 1024, 60, 192], P('tm', 'res')
- grad_message_in: float32 [1216, 512], replicated
- grad_message_mid: float32 [512, 512], replicated
- grad_message_out: float32 [512, 512], replicated
- grad_gain_node: float32 [512], replicated
- grad_offset_node: float32 [512], replicated
- grad_expand: float32 [512, 2048], replicated
- grad_contract: float32 [2048, 512], replicated
- grad_gain_ffn: float32 [512], replicated
- grad_offset_ffn: float32 [512], replicated
- grad_update_in: float32 [1216, 192], replicated
- grad_update_mid: float32 [192, 192], replicated
- grad_update_out: float32 [192, 192], replicated
- grad_gain_edge: float32 [192], replicated
- grad_offset_edge: float32 [192], replicated
Inputs may be any that keep to these rules, and one draw needn't show every extreme that they name: `neighbour`: below 128 an entry names a residue of the own block; an entry s of 128 or more names the residue fetch_rows[block, (s - 128) // 32, (s - 128) % 32]. fetch_rows[d, p] holds 32 distinct residues of block p, that is of p * 128 to (p + 1) * 128 - 1. `chain_ids`: never falls along residues; no chain crosses from one block of 128 residues to the next. `complex_flag`: equal for all residues of a chain; the first chain of every block is in the complex. `edge_mask`: some residues are padding with no live edge.
All inputs are finite; a program needn't handle non-finite values.
Results may differ from a plain program's by a relative error of at most 0.02.
Values may be sent and summed in bfloat16 or wider, within the bound.
A program may use at most 256 MiB of HBM per device.

v0:
```python
import jax
import jax.numpy as jnp
from jax import lax
from jax.sharding import PartitionSpec as P

EPSILON = 1e-05


def activate(values):
    return jax.nn.gelu(values, approximate=True)


def layer_norm(values, gain_vec, offset):
    centred = values - jnp.mean(values, axis=-1, keepdims=True)
    spread = jnp.mean(centred * centred, axis=-1, keepdims=True)
    return centred * lax.rsqrt(spread + EPSILON) * gain_vec + offset


def forward_dot(left_op, right_op):
    return jnp.dot(left_op, right_op, preferred_element_type=jnp.float32)


def weight_grad(inputs, grad_rows):
    return lax.dot_general(
        inputs, grad_rows, (((0,), (0,)), ((), ())), preferred_element_type=jnp.float32
    )


def input_grad(grad_rows, weight):
    return lax.dot_general(
        grad_rows, weight, (((1,), (1,)), ((), ())), preferred_element_type=jnp.float32
    )


def edge_dot(edges, weight):
    return jnp.einsum("rke,ef->rkf", edges, weight, preferred_element_type=jnp.float32)


def edge_weight_grad(edges, grads):
    return jnp.einsum("rke,rkf->ef", edges, grads, preferred_element_type=jnp.float32)


def edge_input_grad(grads, weight):
    return jnp.einsum("rkf,ef->rke", grads, weight, preferred_element_type=jnp.float32)


def through_gate(pre_act, grad_out):
    unused, pullback = jax.vjp(activate, pre_act)
    return pullback(grad_out)[0].astype(jnp.bfloat16)


def one_hot_rows(indices, table_len):
    return (indices[:, None] == jnp.arange(table_len, dtype=jnp.int32)[None, :]).astype(
        jnp.bfloat16
    )


def pick_rows(picker, table):
    upper = table.astype(jnp.bfloat16)
    lower = (table - upper.astype(jnp.float32)).astype(jnp.bfloat16)
    return jnp.einsum(
        "rkl,ld->rkd", picker, upper, preferred_element_type=jnp.float32
    ) + jnp.einsum("rkl,ld->rkd", picker, lower, preferred_element_type=jnp.float32)


def table_grad(picker, grads):
    return jnp.einsum("rkl,rkd->ld", picker, grads, preferred_element_type=jnp.float32)


def message_pass(self_proj, table_proj, picker, edge_in, edge_weight, mid_weight, out_weight):
    gathered = pick_rows(picker, table_proj)
    pre_one = self_proj[:, None, :] + gathered + edge_dot(edge_in, edge_weight)
    hidden_one = activate(pre_one).astype(jnp.bfloat16)
    pre_two = edge_dot(hidden_one, mid_weight)
    hidden_two = activate(pre_two).astype(jnp.bfloat16)
    return (pre_one, hidden_one, pre_two, hidden_two, edge_dot(hidden_two, out_weight))


def local(
    node_feats,
    edge_feats,
    node_cotan,
    edge_cotan,
    neighbour,
    edge_mask,
    fetch_rows,
    chain_ids,
    complex_flag,
    message_in,
    message_mid,
    message_out,
    gain_node,
    offset_node,
    expand_weight,
    contract_weight,
    gain_ffn,
    offset_ffn,
    update_in,
    update_mid,
    update_out,
    gain_edge,
    offset_edge,
):
    row_count, fanout = neighbour.shape
    feat_width = node_feats.shape[2]
    peer_count = fetch_rows.shape[1]
    slot_count = fetch_rows.shape[2]
    table_len = row_count + peer_count * slot_count
    node_in = node_feats[0]
    edge_in = edge_feats[0]
    wanted = fetch_rows[0].reshape(peer_count * slot_count)
    my_index = lax.axis_index("res")
    own_ids = my_index * row_count + jnp.arange(row_count, dtype=jnp.int32)
    table_ids = jnp.concatenate([own_ids, wanted], axis=0)
    tag_local = chain_ids * 2 + complex_flag
    picker = (
        neighbour[:, :, None] == jnp.arange(table_len, dtype=jnp.int32)[None, None, :]
    ).astype(jnp.bfloat16)
    all_rows, all_tags = (
        lax.all_gather(node_in, "res", axis=0, tiled=True),
        lax.all_gather(tag_local, "res", axis=0, tiled=True),
    )
    wanted_picker = one_hot_rows(wanted, peer_count * row_count)
    far_rows = forward_dot(wanted_picker, all_rows).astype(jnp.bfloat16)
    far_tags = jnp.take(all_tags, wanted)
    table_rows = jnp.concatenate([node_in, far_rows], axis=0)
    table_tags = jnp.concatenate([tag_local, far_tags], axis=0)
    other_tag = jnp.take(table_tags, neighbour, axis=0)
    joined = jnp.logical_or(
        chain_ids[:, None] == other_tag // 2, complex_flag[:, None] * (other_tag % 2) > 0
    )
    keep = edge_mask.astype(jnp.float32) * joined.astype(jnp.float32)
    counted = jnp.maximum(jnp.sum(keep, axis=1), 1.0)
    self_weight = message_in[:feat_width]
    neigh_weight = message_in[feat_width : 2 * feat_width]
    message_edge = message_in[2 * feat_width :]
    self_proj = forward_dot(node_in, self_weight)
    table_proj = forward_dot(table_rows, neigh_weight)
    kept = message_pass(
        self_proj, table_proj, picker, edge_in, message_edge, message_mid, message_out
    )
    aggregate = jnp.sum(kept[4] * keep[:, :, None], axis=1) / counted[:, None]
    first, first_pull = jax.vjp(
        layer_norm,
        node_in.astype(jnp.float32) + aggregate,
        gain_node.astype(jnp.float32),
        offset_node.astype(jnp.float32),
    )
    first_low = first.astype(jnp.bfloat16)
    inner = forward_dot(first_low, expand_weight)
    acted = activate(inner).astype(jnp.bfloat16)
    ffn_out = forward_dot(acted, contract_weight)
    updated, second_pull = jax.vjp(
        layer_norm, first + ffn_out, gain_ffn.astype(jnp.float32), offset_ffn.astype(jnp.float32)
    )
    updated_low = updated.astype(jnp.bfloat16)
    far_new = forward_dot(
        wanted_picker, lax.all_gather(updated_low, "res", axis=0, tiled=True)
    ).astype(jnp.bfloat16)
    table_new = jnp.concatenate([updated_low, far_new], axis=0)
    update_self = update_in[:feat_width]
    update_neigh = update_in[feat_width : 2 * feat_width]
    update_edge = update_in[2 * feat_width :]
    self_edge = forward_dot(updated_low, update_self)
    table_edge = forward_dot(table_new, update_neigh)
    gathered_edge = pick_rows(picker, table_edge)
    pre_three = self_edge[:, None, :] + gathered_edge + edge_dot(edge_in, update_edge)
    hidden_three = activate(pre_three).astype(jnp.bfloat16)
    pre_four = edge_dot(hidden_three, update_mid)
    hidden_four = activate(pre_four).astype(jnp.bfloat16)
    branch = edge_dot(hidden_four, update_out)
    edge_new, third_pull = jax.vjp(
        layer_norm,
        edge_in.astype(jnp.float32) + branch,
        gain_edge.astype(jnp.float32),
        offset_edge.astype(jnp.float32),
    )
    delta_resid, grad_gain_edge, grad_offset_edge = third_pull(edge_cotan[0].astype(jnp.float32))
    delta_branch = delta_resid.astype(jnp.bfloat16)
    grad_update_out = edge_weight_grad(hidden_four, delta_branch)
    delta_four = through_gate(pre_four, edge_input_grad(delta_branch, update_out))
    grad_update_mid = edge_weight_grad(hidden_three, delta_four)
    delta_three = through_gate(pre_three, edge_input_grad(delta_four, update_mid))
    grad_update_edge = edge_weight_grad(edge_in, delta_three)
    delta_edge_in = delta_resid + edge_input_grad(delta_three, update_edge)
    delta_self_edge = jnp.sum(delta_three, axis=1, dtype=jnp.float32).astype(jnp.bfloat16)
    delta_table_edge = table_grad(picker, delta_three)
    table_picker = one_hot_rows(table_ids, peer_count * row_count).astype(jnp.float32)
    spread_edge = lax.dot_general(
        table_picker, delta_table_edge, (((0,), (0,)), ((), ())), precision=lax.Precision.HIGHEST
    )
    own_edge = lax.psum_scatter(
        spread_edge.astype(jnp.bfloat16), "res", scatter_dimension=0, tiled=True
    )
    grad_update_self = weight_grad(updated_low, delta_self_edge)
    grad_update_neigh = weight_grad(updated_low, own_edge)
    delta_updated = (
        node_cotan[0].astype(jnp.float32)
        + input_grad(delta_self_edge, update_self)
        + input_grad(own_edge, update_neigh)
    )
    delta_second, grad_gain_ffn, grad_offset_ffn = second_pull(delta_updated)
    delta_ffn = delta_second.astype(jnp.bfloat16)
    grad_contract = weight_grad(acted, delta_ffn)
    delta_inner = through_gate(inner, input_grad(delta_ffn, contract_weight))
    grad_expand = weight_grad(first_low, delta_inner)
    delta_first = delta_second + input_grad(delta_inner, expand_weight)
    delta_first_in, grad_gain_node, grad_offset_node = first_pull(delta_first)
    delta_message = ((delta_first_in / counted[:, None])[:, None, :] * keep[:, :, None]).astype(
        jnp.bfloat16
    )
    pre_one, hidden_one, pre_two, hidden_two, unused_message = kept
    grad_message_out = edge_weight_grad(hidden_two, delta_message)
    delta_two = through_gate(pre_two, edge_input_grad(delta_message, message_out))
    grad_message_mid = edge_weight_grad(hidden_one, delta_two)
    delta_one = through_gate(pre_one, edge_input_grad(delta_two, message_mid))
    grad_message_edge = edge_weight_grad(edge_in, delta_one)
    delta_edge_in = delta_edge_in + edge_input_grad(delta_one, message_edge)
    delta_self = jnp.sum(delta_one, axis=1, dtype=jnp.float32).astype(jnp.bfloat16)
    delta_table = table_grad(picker, delta_one)
    spread_node = lax.dot_general(
        table_picker, delta_table, (((0,), (0,)), ((), ())), precision=lax.Precision.HIGHEST
    )
    own_node = lax.psum_scatter(
        spread_node.astype(jnp.bfloat16), "res", scatter_dimension=0, tiled=True
    )
    grad_message_self = weight_grad(node_in, delta_self)
    grad_message_neigh = weight_grad(node_in, own_node)
    delta_node_in = (
        delta_first_in + input_grad(delta_self, self_weight) + input_grad(own_node, neigh_weight)
    )
    grad_message_in = jnp.concatenate(
        [grad_message_self, grad_message_neigh, grad_message_edge], axis=0
    )
    grad_update_in = jnp.concatenate(
        [grad_update_self, grad_update_neigh, grad_update_edge], axis=0
    )
    totals = lax.psum(
        (
            grad_message_in,
            grad_message_mid,
            grad_message_out,
            grad_gain_node,
            grad_offset_node,
            grad_expand,
            grad_contract,
            grad_gain_ffn,
            grad_offset_ffn,
            grad_update_in,
            grad_update_mid,
            grad_update_out,
            grad_gain_edge,
            grad_offset_edge,
        ),
        ("tm", "res"),
    )
    return (
        updated_low[None],
        edge_new.astype(jnp.bfloat16)[None],
        delta_node_in[None],
        delta_edge_in[None],
        totals[0],
        totals[1],
        totals[2],
        totals[3],
        totals[4],
        totals[5],
        totals[6],
        totals[7],
        totals[8],
        totals[9],
        totals[10],
        totals[11],
        totals[12],
        totals[13],
    )


def solution(mesh):
    placed = (
        P("tm", "res", None),
        P("tm", "res", None, None),
        P("tm", "res", None),
        P("tm", "res", None, None),
        P("res", None),
        P("res", None),
        P("res", None, None),
        P("res"),
        P("res"),
        P(),
        P(),
        P(),
        P(),
        P(),
        P(),
        P(),
        P(),
        P(),
        P(),
        P(),
        P(),
        P(),
        P(),
    )
    return jax.shard_map(
        local,
        mesh=mesh,
        in_specs=placed,
        out_specs=(
            P("tm", "res", None),
            P("tm", "res", None, None),
            P("tm", "res", None),
            P("tm", "res", None, None),
            P(),
            P(),
            P(),
            P(),
            P(),
            P(),
            P(),
            P(),
            P(),
            P(),
            P(),
            P(),
            P(),
            P(),
        ),
        check_vma=False,
    )
```

profile of v0, /device:TPU:0, one launch (start us, length us, event | category | flops | bytes accessed | tf_op | source)
XLA Modules:
  0.0 621.4 jit_solution(12304324607836840426)
XLA Ops:
  13.0 13.4 %all-gather.1 = s32[8,1,128]{2,1,0:T(1,128)S(1)} all-gather(s32[1,1,128]{2,1,0:T(1,128)S(1)} %bitcast.183), channel_id=1, replica_groups=mesh['tm'=4,'res'=8] {'res'}, dimensions={0}, use_global_device_ids=true | all-gather | bytes 4608 | tf_op jit(solution)/shard_map/all_gather | solution.py:121
  28.8 45.2 %gather_fusion.1 = s32[7680]{0:T(1024)S(1)} fusion(s32[384]{0:T(512)S(1)} %pad_add_fusion, s32[8192]{0:T(1024)S(1)} %pad_clamp_fusion), kind=kCustom, calls=%fused_computation.1 | custom fusion | bytes 92160 | tf_op jit(solution)/shard_map/jit(_take)/gather | solution.py:128
  75.8 9.6 %fusion.58 = f32[128,60,512]{2,0,1:T(8,128)} fusion(bf16[1,128,60,192]{1,3,2,0:T(8,128)(2,1)} %param.24, bf16[1216,512]{1,0:T(8,128)(2,1)} %param.32), kind=kOutput, calls=%fused_computation.85 | convolution fusion | flops 1509949440 | bytes 18874368 | tf_op jit(solution)/shard_map/rke,ef->rkf/dot_general | solution.py:36
  88.6 7.7 %fusion.18 = f32[128,60,512]{2,0,1:T(8,128)} fusion(s32[128,60]{0,1:T(8,128)S(1)} %copy-done.24, f32[384,512]{1,0:T(8,128)S(1)} %fusion.94), kind=kOutput, calls=%fused_computation.30 | convolution fusion | flops 3023634432 | bytes 16545792 | tf_op jit(solution)/shard_map/rkl,ld->rkd/dot_general | solution.py:63
  96.3 17.7 %add_add_fusion = f32[128,60,512]{2,0,1:T(8,128)} fusion(f32[128,60,512]{2,0,1:T(8,128)} %fusion.58, f32[128,60,512]{2,0,1:T(8,128)} %fusion.18, f32[128,512]{1,0:T(8,128)S(1)} %fusion.97, s32[128,60]{0,1:T(8,128)S(1)} %copy-done.24, f32[384,512]{1,0:T(8,128)S(1)} %fusion.94), kind=kOutput, calls=%fused_computation.24 | convolution fusion | flops 3034841088 | bytes 48265216 | tf_op jit(solution)/shard_map/rkl,ld->rkd/dot_general | solution.py:61
  114.0 16.2 %multiply_convert_fusion.1 = (bf16[128,60,512]{2,0,1:T(8,128)(2,1)S(1)}, f32[128,60,512]{2,0,1:T(8,128)}) fusion(bf16[512,512]{1,0:T(8,128)(2,1)} %param.33, f32[128,60,512]{2,0,1:T(8,128)} %add_add_fusion), kind=kOutput, calls=%fused_computation.22 | convolution fusion | flops 4097310720 | bytes 39845888 | tf_op jit(solution)/shard_map/rke,ef->rkf/dot_general | solution.py:36
  130.2 4.5 multiply_reduce_fusion
  139.7 19.2 %all-gather.5.cloned.1.call-done = bf16[1024,512]{1,0:T(8,128)(2,1)} async-done(((bf16[128,512]{1,0:T(8,128)(2,1)}), bf16[1024,512]{1,0:T(8,128)(2,1)}) %all-gather.5.cloned.1.call-update) | async-done | bytes 1048592 | tf_op jit(solution)/shard_map/all_gather | solution.py:158
  168.5 3.3 fusion.128
  171.9 3.1 fusion.161
  177.6 6.6 %fusion.30 = (f32[192]{0:T(256)}, f32[128,60]{0,1:T(8,128)S(1)}, bf16[1,128,60,192]{1,3,2,0:T(8,128)(2,1)}) fusion(bf16[1,128,60,192]{1,3,2,0:T(8,128)(2,1)S(1)} %copy-done.3, f32[128,60,192]{0,2,1:T(8,128)S(1)} %get-tuple-element.58, f32[128,60]{0,1:T(8,128)S(1)} %get-tuple-element.52, f32[128,60]{0,1:T(8,128)S(1)} %broadcast_multiply_fusion, ...), kind=kLoop, calls=%fused_computation.49 | loop fusion | flops 20635968 | bytes 11921664 | tf_op jit(solution)/shard_map/transpose(jvp())/reduce_sum | solution.py:16
  184.2 4.3 convolution_bitcast_fusion.3
  188.6 6.4 %fusion.44 = bf16[128,60,192]{0,2,1:T(8,128)(2,1)S(1)} fusion(f32[128,60,192]{0,2,1:T(8,128)S(1)} %fusion.128, f32[128,60]{0,1:T(8,128)S(1)} %negate_multiply_fusion, bf16[192,192]{1,0:T(8,128)(2,1)S(1)} %copy-done.87, bf16[1,128,60,192]{1,3,2,0:T(8,128)(2,1)S(1)} %copy-done.3, f32[128,60,192]{0,2,1:T(8,128)S(1)} %get-tuple-element.58, ...), kind=kOutput, calls=%fused_computation.63 | convolution fusion | flops 608993280 | bytes 17892096 | tf_op jit(solution)/shard_map/rkf,ef->rke/dot_general | solution.py:44
  195.0 5.0 fusion.162
  209.9 6.2 %convolution_bitcast_fusion.4 = f32[192,192]{1,0:T(8,128)} fusion(bf16[128,60,192]{0,2,1:T(8,128)(2,1)} %copy-done.92, f32[128,60,192]{0,2,1:T(8,128)} %copy-done.9), kind=kOutput, calls=%fused_computation.113 | convolution fusion | flops 579502080 | bytes 8994816 | tf_op jit(solution)/shard_map/rke,rkf->ef/dot_general | solution.py:40
  216.2 22.4 %reduce-scatter.7.cloned.1.call-done = bf16[128,192]{1,0:T(8,128)(2,1)} async-done(((bf16[1024,192]{1,0:T(8,128)(2,1)}), bf16[128,192]{1,0:T(8,128)(2,1)}) %reduce-scatter.7.cloned.1.call-update) | async-done | bytes 49168
  240.6 2.9 fusion.82
  245.4 8.7 %fusion.65 = f32[512,512]{1,0:T(8,128)} fusion(bf16[128,60,512]{2,0,1:T(8,128)(2,1)} %copy-done.91, f32[128,512]{1,0:T(8,128)S(1)} %add_divide_fusion, f32[128,60]{0,1:T(8,128)S(1)} %copy-done.49), kind=kOutput, calls=%fused_computation.94 | convolution fusion | flops 4034396160 | bytes 9205760 | tf_op jit(solution)/shard_map/rke,rkf->ef/dot_general | solution.py:40
  254.1 17.7 %fusion.13 = bf16[128,60,512]{2,0,1:T(8,128)(2,1)} fusion(f32[128,60,512]{2,0,1:T(8,128)} %get-tuple-element.54, f32[128,512]{1,0:T(8,128)S(1)} %add_divide_fusion, f32[128,60]{0,1:T(8,128)S(1)} %copy-done.49, bf16[512,512]{1,0:T(8,128)(2,1)S(1)} %copy-done.85), kind=kOutput, calls=%fused_computation.19 | convolution fusion | flops 4113039360 | bytes 24410112 | tf_op jit(solution)/shard_map/rkf,ef->rke/dot_general | solution.py:44
  271.9 15.9 %fusion.163 = (bf16[128,512]{1,0:T(8,128)(2,1)S(1)}, bf16[128,60,512]{2,0,1:T(8,128)(2,1)S(1)}) fusion(f32[128,60,512]{2,0,1:T(8,128)S(1)} %bitcast.180, bf16[128,60,512]{2,0,1:T(8,128)(2,1)} %fusion.13, bf16[512,512]{1,0:T(8,128)(2,1)S(1)} %copy-done.86), kind=kOutput, calls=%fused_computation.246 | convolution fusion | flops 4109041664 | bytes 32112640 | tf_op jit(solution)/shard_map/rkf,ef->rke/dot_general | solution.py:44
  287.9 6.5 %fusion.68 = f32[192,512]{1,0:T(8,128)} fusion(bf16[128,60,512]{2,0,1:T(8,128)(2,1)S(1)} %get-tuple-element.64, bf16[1,128,60,192]{1,3,2,0:T(8,128)(2,1)} %param.24), kind=kOutput, calls=%fused_computation.100 | convolution fusion | flops 1509949440 | bytes 11206656 | tf_op jit(solution)/shard_map/rke,rkf->ef/dot_general | solution.py:40
  294.4 3.2 fusion.66
  297.6 2.8 fusion.149
  300.4 2.8 fusion.151
  303.3 2.9 fusion.64
  307.9 12.3 %convolution_bitcast_fusion = f32[512,512]{1,0:T(8,128)} fusion(bf16[128,60,512]{2,0,1:T(8,128)(2,1)} %fusion.13, f32[128,60,512]{2,0,1:T(8,128)} %add_add_fusion), kind=kOutput, calls=%fused_computation.95 | convolution fusion | flops 4061921280 | bytes 24641536 | tf_op jit(solution)/shard_map/rke,rkf->ef/dot_general | solution.py:40
  320.2 16.6 %reduce-scatter.5.cloned.1.call-done = bf16[128,512]{1,0:T(8,128)(2,1)} async-done(((bf16[1024,512]{1,0:T(8,128)(2,1)}), bf16[128,512]{1,0:T(8,128)(2,1)}) %reduce-scatter.5.cloned.1.call-update) | async-done | bytes 131088 | tf_op jit(solution)/shard_map/reduce_scatter | solution.py:224
  343.1 40.1 %all-reduce = (f32[512]{0:T(512)}, f32[512]{0:T(512)}, f32[512]{0:T(512)}, f32[512]{0:T(512)}, f32[192]{0:T(256)}, /*index=5*/f32[192]{0:T(256)}) all-reduce(f32[512]{0:T(512)S(1)} %copy-done.66, f32[512]{0:T(512)S(1)} %copy-done.67, f32[512]{0:T(512)S(1)} %copy-done.64, ...), channel_id=1, replica_groups=mesh['tm'=4,'res'=8] {'tm','res'}, use_global_device_ids=true, to_apply=%region_22.23 | all-reduce | flops 2432 | bytes 19456 | tf_op jit(solution)/shard_map/psum | solution.py:238
  383.6 5.4 fusion.110
  389.5 6.5 %add_bitcast_fusion = f32[1,128,60,192]{1,3,2,0:T(8,128)} fusion(f32[128,60,192]{0,2,1:T(8,128)S(1)} %fusion.110, f32[128,60]{0,1:T(8,128)S(1)} %copy-done.41, bf16[128,60,192]{0,2,1:T(8,128)(2,1)S(1)} %copy-done.19, bf16[1216,192]{0,1:T(8,128)(2,1)} %param.41, f32[128,60]{0,1:T(8,128)S(1)} %copy-done.33, f32[128,60,192]{0,2,1:T(8,128)} %copy-done.2, ...), kind=kOutput, calls=%fused_computation.64 | convolution fusion | flops 580976640 | bytes 23814912 | tf_op jit(solution)/shard_map/rkf,ef->rke/dot_general | solution.py:44
  397.1 204.0 %all-reduce.4.cloned.1.call-done = (f32[1216,512]{1,0:T(8,128)}, f32[512,512]{1,0:T(8,128)}, f32[512,512]{1,0:T(8,128)}, f32[512,2048]{1,0:T(8,128)}, f32[2048,5...) async-done(((f32[1216,512]{1,0:T(8,128)}, f32[512,512]{1,0:T(8,128)}, f32[512,512]{1,0:T(8,128)}, f32[512,2048]{1,0:T(8,128)}, ...) | async-done | bytes 14204944 | tf_op jit(solution)/shard_map/psum | solution.py:238
  601.1 3.5 copy.94
  (285 shorter events, 62.9 us)
Async XLA Ops:
  7.2 128.0 %copy-start = (bf16[512,2048]{1,0:T(8,128)(2,1)S(1)}, bf16[512,2048]{1,0:T(8,128)(2,1)}, u32[]{:S(2)}) copy-start(bf16[512,2048]{1,0:T(8,128)(2,1)} %param.37) | copy-start | bytes 6291460
  7.2 78.2 %all-gather.7.cloned.1.call-start = ((), (), s32[]{:S(2)}) async-start(), calls=%async_computation.4 | async-start | bytes 1179648 | tf_op jit(solution)/shard_map/all_gather | solution.py:120
  7.9 150.9 %all-gather.5.cloned.1.call-start = ((), (), s32[]{:S(2)}) async-start(), calls=%async_computation.2 | async-start | bytes 1179648 | tf_op jit(solution)/shard_map/all_gather | solution.py:158
  10.2 125.5 %copy-start.45 = (f32[512]{0:T(512)}, f32[512]{0:T(512)S(1)}, u32[]{:S(2)}) copy-start(f32[512]{0:T(512)S(1)} %convert_element_type.134) | copy-start | bytes 6148
  10.9 126.7 %copy-start.42 = (f32[512]{0:T(512)}, f32[512]{0:T(512)S(1)}, u32[]{:S(2)}) copy-start(f32[512]{0:T(512)S(1)} %convert_element_type.138) | copy-start | bytes 6148
  11.6 124.1 %copy-start.52 = (f32[512]{0:T(512)}, f32[512]{0:T(512)S(1)}, u32[]{:S(2)}) copy-start(f32[512]{0:T(512)S(1)} %convert_element_type.135) | copy-start | bytes 6148
  12.3 125.3 %copy-start.50 = (f32[512]{0:T(512)}, f32[512]{0:T(512)S(1)}, u32[]{:S(2)}) copy-start(f32[512]{0:T(512)S(1)} %convert_element_type.139) | copy-start | bytes 6148
  28.7 45.4 %copy-start.47 = (s32[128,60]{0,1:T(8,128)S(1)}, s32[128,60]{0,1:T(8,128)}, u32[]{:S(2)}) copy-start(s32[128,60]{0,1:T(8,128)} %param.28) | copy-start | bytes 92164
  28.7 45.5 %copy-start.77 = (s32[128]{0:T(128)S(1)}, s32[128]{0:T(128)}, u32[]{:S(2)}) copy-start(s32[128]{0:T(128)} %param.31) | copy-start | bytes 1540
  28.7 45.5 %copy-start.78 = (s32[128]{0:T(128)S(1)}, s32[128]{0:T(128)}, u32[]{:S(2)}) copy-start(s32[128]{0:T(128)} %param.30) | copy-start | bytes 1540
  28.8 45.8 %copy-start.14 = (bf16[1,128,512]{2,1,0:T(8,128)(2,1)S(1)}, bf16[1,128,512]{2,1,0:T(8,128)(2,1)}, u32[]{:S(2)}) copy-start(bf16[1,128,512]{2,1,0:T(8,128)(2,1)} %param.23) | copy-start | bytes 393220
  74.5 55.7 %copy-start.48 = (f32[128,60]{0,1:T(8,128)}, f32[128,60]{0,1:T(8,128)S(1)}, u32[]{:S(2)}) copy-start(f32[128,60]{0,1:T(8,128)S(1)} %copy.62) | copy-start | bytes 92164
  74.6 60.2 %copy-start.73 = (f32[128]{0:T(128)}, f32[128]{0:T(128)S(1)}, u32[]{:S(2)}) copy-start(f32[128]{0:T(128)S(1)} %broadcast_maximum_fusion) | copy-start | bytes 1540
  137.3 103.0 %copy-start.7 = (f32[128,512]{1,0:T(8,128)}, f32[128,512]{1,0:T(8,128)S(1)}, u32[]{:S(2)}) copy-start(f32[128,512]{1,0:T(8,128)S(1)} %get-tuple-element.56) | copy-start | bytes 786436
  137.4 29.6 %copy-start.54 = (f32[128]{0:T(128)}, f32[128]{0:T(128)S(1)}, u32[]{:S(2)}) copy-start(f32[128]{0:T(128)S(1)} %broadcast_multiply_fusion.1) | copy-start | bytes 1540
  137.6 29.4 %copy-start.81 = (f32[128]{0:T(128)}, f32[128]{0:T(128)S(1)}, u32[]{:S(2)}) copy-start(f32[128]{0:T(128)S(1)} %multiply_reduce_fusion.6) | copy-start | bytes 1540
  137.6 29.4 %copy-start.61 = (f32[128]{0:T(128)}, f32[128]{0:T(128)S(1)}, u32[]{:S(2)}) copy-start(f32[128]{0:T(128)S(1)} %fusion.143) | copy-start | bytes 1540
  138.4 100.2 %reduce-scatter.7.cloned.1.call-start = ((), (), s32[]{:S(2)}) async-start(), calls=%async_computation.5 | async-start | bytes 589824
  138.5 50.0 %copy-start.59 = (f32[192]{0:T(256)}, f32[192]{0:T(256)S(1)}, u32[]{:S(2)}) copy-start(f32[192]{0:T(256)S(1)} %convert_element_type.148) | copy-start | bytes 2308
  138.6 65.5 %copy-start.71 = (s32[384]{0:T(512)}, s32[384]{0:T(512)S(1)}, u32[]{:S(2)}) copy-start(s32[384]{0:T(512)S(1)} %pad_add_fusion.1) | copy-start | bytes 4612
  207.8 129.0 %reduce-scatter.5.cloned.1.call-start = ((), (), s32[]{:S(2)}) async-start(), calls=%async_computation.3 | async-start | bytes 1179648 | tf_op jit(solution)/shard_map/reduce_scatter | solution.py:224
  209.9 28.7 %copy-start.43 = (f32[512]{0:T(512)S(1)}, f32[512]{0:T(512)}, u32[]{:S(2)}) copy-start(f32[512]{0:T(512)} %copy-done.42) | copy-start | bytes 6148
  209.9 28.7 %copy-start.55 = (f32[128]{0:T(128)S(1)}, f32[128]{0:T(128)}, u32[]{:S(2)}) copy-start(f32[128]{0:T(128)} %copy-done.54) | copy-start | bytes 1540
  209.9 28.7 %copy-start.62 = (f32[128]{0:T(128)S(1)}, f32[128]{0:T(128)}, u32[]{:S(2)}) copy-start(f32[128]{0:T(128)} %copy-done.61) | copy-start | bytes 1540
  209.9 30.4 %copy-start.82 = (f32[128]{0:T(128)S(1)}, f32[128]{0:T(128)}, u32[]{:S(2)}) copy-start(f32[128]{0:T(128)} %copy-done.81) | copy-start | bytes 1540
  216.2 27.4 %copy-start.69 = (f32[128]{0:T(128)S(1)}, f32[128]{0:T(128)}, u32[]{:S(2)}) copy-start(f32[128]{0:T(128)} %copy-done.68) | copy-start | bytes 1540
  216.2 28.8 %copy-start.80 = (f32[128]{0:T(128)S(1)}, f32[128]{0:T(128)}, u32[]{:S(2)}) copy-start(f32[128]{0:T(128)} %copy-done.79) | copy-start | bytes 1540
  306.2 294.9 %all-reduce.4.cloned.1.call-start = ((), (), s32[]{:S(2)}) async-start(), calls=%async_computation.6 | async-start | bytes 28704768 | tf_op jit(solution)/shard_map/psum | solution.py:238
  307.9 30.1 %copy-start.31 = (f32[192,512]{1,0:T(8,128)S(1)}, f32[192,512]{1,0:T(8,128)}, u32[]{:S(2)}) copy-start(f32[192,512]{1,0:T(8,128)} %fusion.68) | copy-start | bytes 1179652
  339.8 43.5 %copy-start.17 = (bf16[1216,512]{1,0:T(8,128)(2,1)S(1)}, bf16[1216,512]{1,0:T(8,128)(2,1)}, u32[]{:S(2)}) copy-start(bf16[1216,512]{1,0:T(8,128)(2,1)} %param.32) | copy-start | bytes 3735556
  339.8 43.5 %copy-start.21 = (f32[128,512]{1,0:T(8,128)S(1)}, f32[128,512]{1,0:T(8,128)}, u32[]{:S(2)}) copy-start(f32[128,512]{1,0:T(8,128)} %copy-done.20) | copy-start | bytes 786436
  339.8 43.5 %copy-start.76 = (f32[128]{0:T(128)S(1)}, f32[128]{0:T(128)}, u32[]{:S(2)}) copy-start(f32[128]{0:T(128)} %copy-done.75) | copy-start | bytes 1540
  (70 other events, 572.0 us)
Sparse Core Ops, SparseCore 0:
  9.6 24.7 all-gather.6
  138.5 20.3 all-gather.4
  207.9 30.6 reduce-scatter.6
  306.3 30.3 reduce-scatter.4
  345.3 255.7 all-reduce.3
where the time goes:
time: 629 us; the launch traced here: 621 us
  waiting for transfers between devices  263 us (42%)
  matrix products  202 us (32%)
  local copies, waits for them, and re-layouts  66.6 us (11%)
  blocking collectives  53.5 us (9%)
  other arithmetic  20.6 us (3%)
  between operations  15.6 us (2%)
    psum x1, waiting for transfers between devices, local(): lax.psum((grad_message_in, grad_message_mid, grad_message_out, grad_gain_...  204 us
    dot_general x6, matrix products, edge_input_grad(): jnp.einsum('rkf,ef->rke', grads, weight, preferred_element_type=jnp.float32)  57 us
    gather x2, local copies, waits for them, and re-layouts, local(): other_tag = jnp.take(table_tags, neighbour, axis=0)  45.3 us
    psum x1, blocking collectives, local(): lax.psum((grad_message_in, grad_message_mid, grad_message_out, grad_gain_...  40.1 us
    dot_general x6, matrix products, edge_weight_grad(): jnp.einsum('rke,rkf->ef', edges, grads, preferred_element_type=jnp.float32)  39.7 us
    dot_general x6, matrix products, edge_dot(): jnp.einsum('rke,ef->rkf', edges, weight, preferred_element_type=jnp.float32)  38.1 us
    unnamed x6, waiting for transfers between devices  23.2 us
    dot_general x2, matrix products, pick_rows(): jnp.einsum('rkl,ld->rkd', picker, upper, preferred_element_type=jnp.float32)  20.2 us
  transfers between devices with their start and end apart: 5, of which 4 were waited for; matrix products, arithmetic and copies ran while one was open for 17% of the time, Pallas kernels for 0%

commit v1 on v0

--- a/solution.py
+++ b/solution.py
@@ -236,23 +236,26 @@
         [grad_update_self, grad_update_neigh, grad_update_edge], axis=0
     )
     totals = lax.psum(
-        (
-            grad_message_in,
-            grad_message_mid,
-            grad_message_out,
-            grad_gain_node,
-            grad_offset_node,
-            grad_expand,
-            grad_contract,
-            grad_gain_ffn,
-            grad_offset_ffn,
-            grad_update_in,
-            grad_update_mid,
-            grad_update_out,
-            grad_gain_edge,
-            grad_offset_edge,
+        lax.psum(
+            (
+                grad_message_in,
+                grad_message_mid,
+                grad_message_out,
+                grad_gain_node,
+                grad_offset_node,
+                grad_expand,
+                grad_contract,
+                grad_gain_ffn,
+                grad_offset_ffn,
+                grad_update_in,
+                grad_update_mid,
+                grad_update_out,
+                grad_gain_edge,
+                grad_offset_edge,
+            ),
+            "res",
         ),
-        ("tm", "res"),
+        "tm",
     )
     return (
         updated_low[None],

time: 629 us -> 938 us (1.49)
  waiting for transfers between devices: 263 us -> 566 us
    psum x0 -> x1, waiting for transfers between devices: none -> 217 us  [local(): lax.psum(lax.psum((grad_message_in, grad_message_mid, grad_message_out, g...]
    psum x1, waiting for transfers between devices: 204 us -> 290 us  [local(): lax.psum((grad_message_in, grad_message_mid, grad_message_out, grad_gain_...]
    psum x0 -> x1, blocking collectives: none -> 17.4 us  [local(): lax.psum(lax.psum((grad_message_in, grad_message_mid, grad_message_out, g...]
    psum x1, blocking collectives: 40.1 us -> 28 us  [local(): lax.psum((grad_message_in, grad_message_mid, grad_message_out, grad_gain_...]
    unnamed x6 -> x7, waiting for transfers between devices: 23.2 us -> 23.2 us
  transfers between devices with their start and end apart: 5 -> 6, of which waited for: 4 -> 5; matrix products, arithmetic and copies ran while one was open for 17% -> 11% of each run, Pallas kernels for 0% -> 0%
where the time goes in v1:
time: 938 us; the launch traced here: 930 us
  waiting for transfers between devices  566 us (60%)
  matrix products  202 us (22%)
  local copies, waits for them, and re-layouts  66.1 us (7%)
  blocking collectives  58.7 us (6%)
  other arithmetic  20.6 us (2%)
  between operations  16 us (2%)
    psum x1, waiting for transfers between devices, local(): lax.psum((grad_message_in, grad_message_mid, grad_message_out, grad_gain_...  290 us
    psum x1, waiting for transfers between devices, local(): lax.psum(lax.psum((grad_message_in, grad_message_mid, grad_message_out, g...  217 us
    dot_general x6, matrix products, edge_input_grad(): jnp.einsum('rkf,ef->rke', grads, weight, preferred_element_type=jnp.float32)  57.2 us
    gather x2, local copies, waits for them, and re-layouts, local(): other_tag = jnp.take(table_tags, neighbour, axis=0)  45.3 us
    dot_general x6, matrix products, edge_weight_grad(): jnp.einsum('rke,rkf->ef', edges, grads, preferred_element_type=jnp.float32)  39.7 us
    dot_general x6, matrix products, edge_dot(): jnp.einsum('rke,ef->rkf', edges, weight, preferred_element_type=jnp.float32)  38.1 us
    psum x1, blocking collectives, local(): lax.psum((grad_message_in, grad_message_mid, grad_message_out, grad_gain_...  28 us
    unnamed x7, waiting for transfers between devices  23.2 us
  transfers between devices with their start and end apart: 6, of which 5 were waited for; matrix products, arithmetic and copies ran while one was open for 11% of the time, Pallas kernels for 0%

profile of v1, /device:TPU:0, one launch (start us, length us, event | category | flops | bytes accessed | tf_op | source)
XLA Modules:
  0.0 929.9 jit_solution(4560519678609903173)
XLA Ops:
  13.0 13.4 %all-gather.1 = s32[8,1,128]{2,1,0:T(1,128)S(1)} all-gather(s32[1,1,128]{2,1,0:T(1,128)S(1)} %bitcast.183), channel_id=1, replica_groups=mesh['tm'=4,'res'=8] {'res'}, dimensions={0}, use_global_device_ids=true | all-gather | bytes 4608 | tf_op jit(solution)/shard_map/all_gather | solution.py:121
  28.8 45.2 %gather_fusion.1 = s32[7680]{0:T(1024)S(1)} fusion(s32[384]{0:T(512)S(1)} %pad_add_fusion, s32[8192]{0:T(1024)S(1)} %pad_clamp_fusion), kind=kCustom, calls=%fused_computation.1 | custom fusion | bytes 92160 | tf_op jit(solution)/shard_map/jit(_take)/gather | solution.py:128
  75.8 9.6 %fusion.58 = f32[128,60,512]{2,0,1:T(8,128)} fusion(bf16[1,128,60,192]{1,3,2,0:T(8,128)(2,1)} %param.24, bf16[1216,512]{1,0:T(8,128)(2,1)} %param.32), kind=kOutput, calls=%fused_computation.85 | convolution fusion | flops 1509949440 | bytes 18874368 | tf_op jit(solution)/shard_map/rke,ef->rkf/dot_general | solution.py:36
  88.6 7.7 fusion.18
  96.3 17.7 %add_add_fusion = f32[128,60,512]{2,0,1:T(8,128)} fusion(f32[128,60,512]{2,0,1:T(8,128)} %fusion.58, f32[128,60,512]{2,0,1:T(8,128)} %fusion.18, f32[128,512]{1,0:T(8,128)S(1)} %fusion.97, s32[128,60]{0,1:T(8,128)S(1)} %copy-done.24, f32[384,512]{1,0:T(8,128)S(1)} %fusion.94), kind=kOutput, calls=%fused_computation.24 | convolution fusion | flops 3034841088 | bytes 48265216 | tf_op jit(solution)/shard_map/rkl,ld->rkd/dot_general | solution.py:61
  114.0 16.2 %multiply_convert_fusion.1 = (bf16[128,60,512]{2,0,1:T(8,128)(2,1)S(1)}, f32[128,60,512]{2,0,1:T(8,128)}) fusion(bf16[512,512]{1,0:T(8,128)(2,1)} %param.33, f32[128,60,512]{2,0,1:T(8,128)} %add_add_fusion), kind=kOutput, calls=%fused_computation.22 | convolution fusion | flops 4097310720 | bytes 39845888 | tf_op jit(solution)/shard_map/rke,ef->rkf/dot_general | solution.py:36
  130.2 4.5 multiply_reduce_fusion
  139.7 19.2 %all-gather.5.cloned.1.call-done = bf16[1024,512]{1,0:T(8,128)(2,1)} async-done(((bf16[128,512]{1,0:T(8,128)(2,1)}), bf16[1024,512]{1,0:T(8,128)(2,1)}) %all-gather.5.cloned.1.call-update) | async-done | bytes 1048592 | tf_op jit(solution)/shard_map/all_gather | solution.py:158
  168.5 3.3 fusion.128
  171.9 3.1 fusion.161
  177.6 6.6 fusion.30
  184.2 4.3 convolution_bitcast_fusion.3
  188.6 6.4 fusion.44
  195.0 5.0 fusion.162
  209.9 6.2 convolution_bitcast_fusion.4
  216.2 22.4 %reduce-scatter.7.cloned.1.call-done = bf16[128,192]{1,0:T(8,128)(2,1)} async-done(((bf16[1024,192]{1,0:T(8,128)(2,1)}), bf16[128,192]{1,0:T(8,128)(2,1)}) %reduce-scatter.7.cloned.1.call-update) | async-done | bytes 49168
  240.6 2.9 fusion.82
  245.4 8.7 fusion.65
  254.1 17.7 %fusion.13 = bf16[128,60,512]{2,0,1:T(8,128)(2,1)} fusion(f32[128,60,512]{2,0,1:T(8,128)} %get-tuple-element.68, f32[128,512]{1,0:T(8,128)S(1)} %add_divide_fusion, f32[128,60]{0,1:T(8,128)S(1)} %copy-done.49, bf16[512,512]{1,0:T(8,128)(2,1)S(1)} %copy-done.85), kind=kOutput, calls=%fused_computation.19 | convolution fusion | flops 4113039360 | bytes 24410112 | tf_op jit(solution)/shard_map/rkf,ef->rke/dot_general | solution.py:44
  271.9 15.9 %fusion.163 = (bf16[128,512]{1,0:T(8,128)(2,1)S(1)}, bf16[128,60,512]{2,0,1:T(8,128)(2,1)S(1)}) fusion(f32[128,60,512]{2,0,1:T(8,128)S(1)} %bitcast.180, bf16[128,60,512]{2,0,1:T(8,128)(2,1)} %fusion.13, bf16[512,512]{1,0:T(8,128)(2,1)S(1)} %copy-done.86), kind=kOutput, calls=%fused_computation.246 | convolution fusion | flops 4109041664 | bytes 32112640 | tf_op jit(solution)/shard_map/rkf,ef->rke/dot_general | solution.py:44
  287.8 6.5 fusion.68
  294.4 3.2 fusion.66
  303.3 2.9 fusion.64
  307.8 12.3 %convolution_bitcast_fusion = f32[512,512]{1,0:T(8,128)} fusion(bf16[128,60,512]{2,0,1:T(8,128)(2,1)} %fusion.13, f32[128,60,512]{2,0,1:T(8,128)} %add_add_fusion), kind=kOutput, calls=%fused_computation.95 | convolution fusion | flops 4061921280 | bytes 24641536 | tf_op jit(solution)/shard_map/rke,rkf->ef/dot_general | solution.py:40
  320.2 16.6 %reduce-scatter.5.cloned.1.call-done = bf16[128,512]{1,0:T(8,128)(2,1)} async-done(((bf16[1024,512]{1,0:T(8,128)(2,1)}), bf16[128,512]{1,0:T(8,128)(2,1)}) %reduce-scatter.5.cloned.1.call-update) | async-done | bytes 131088 | tf_op jit(solution)/shard_map/reduce_scatter | solution.py:224
  339.7 290.1 %all-reduce.7.cloned.1.call-done = (f32[1216,512]{1,0:T(8,128)}, f32[512,512]{1,0:T(8,128)}, f32[512,512]{1,0:T(8,128)}, f32[512,2048]{1,0:T(8,128)}, f32[2048,5...) async-done(((f32[1216,512]{1,0:T(8,128)}, f32[512,512]{1,0:T(8,128)}, f32[512,512]{1,0:T(8,128)}, f32[512,2048]{1,0:T(8,128)}, ...) | async-done | bytes 14204944 | tf_op jit(solution)/shard_map/psum | solution.py:239
  633.3 28.0 %all-reduce = (f32[512]{0:T(512)S(1)}, f32[512]{0:T(512)S(1)}, f32[512]{0:T(512)S(1)}, f32[512]{0:T(512)S(1)}, f32[192]{0:T(256)S(1)}, /*index=5*/f32[192]{0:T(256)S(1)}) all-reduce(f32[512]{0:T(512)S(1)} %copy-done.66, f32[512]{0:T(512)S(1)} %copy-done.67, f32[512]{0:T(512)S(1)} %copy-done.64, ...), channel_id=1, replica_groups=mesh['tm'=4,'res'=8] {'res'}, use_global_device_ids=true, to_apply=%region_25.26 | all-reduce | flops 2432 | bytes 19456 | tf_op jit(solution)/shard_map/psum | solution.py:239
  661.3 17.4 %all-reduce.2 = (f32[512]{0:T(512)}, f32[512]{0:T(512)}, f32[512]{0:T(512)}, f32[512]{0:T(512)}, f32[192]{0:T(256)}, /*index=5*/f32[192]{0:T(256)}) all-reduce(f32[512]{0:T(512)S(1)} %get-tuple-element.28, f32[512]{0:T(512)S(1)} %get-tuple-element.29, f32[512]{0:T(512)S(1)} %get-tuple-element.30, ...), channel_id=1, replica_groups=mesh['tm'=4,'res'=8] {'tm'}, use_global_device_ids=true, to_apply=%region_26.27 | all-reduce | flops 2432 | bytes 19456 | tf_op jit(solution)/shard_map/psum | solution.py:238
  679.0 5.5 fusion.110
  684.7 6.6 add_bitcast_fusion
  692.3 216.9 %all-reduce.9.cloned.1.call-done = (f32[1216,512]{1,0:T(8,128)}, f32[512,512]{1,0:T(8,128)}, f32[512,512]{1,0:T(8,128)}, f32[512,2048]{1,0:T(8,128)}, f32[2048,5...) async-done(((f32[1216,512]{1,0:T(8,128)}, f32[512,512]{1,0:T(8,128)}, f32[512,512]{1,0:T(8,128)}, f32[512,2048]{1,0:T(8,128)}, ...) | async-done | bytes 14204944 | tf_op jit(solution)/shard_map/psum | solution.py:238
  909.3 3.5 copy.102
  (289 shorter events, 68.2 us)
Async XLA Ops:
  7.2 128.0 %copy-start = (bf16[512,2048]{1,0:T(8,128)(2,1)S(1)}, bf16[512,2048]{1,0:T(8,128)(2,1)}, u32[]{:S(2)}) copy-start(bf16[512,2048]{1,0:T(8,128)(2,1)} %param.37) | copy-start | bytes 6291460
  7.2 78.2 %all-gather.7.cloned.1.call-start = ((), (), s32[]{:S(2)}) async-start(), calls=%async_computation.4 | async-start | bytes 1179648 | tf_op jit(solution)/shard_map/all_gather | solution.py:120
  7.9 150.9 %all-gather.5.cloned.1.call-start = ((), (), s32[]{:S(2)}) async-start(), calls=%async_computation.2 | async-start | bytes 1179648 | tf_op jit(solution)/shard_map/all_gather | solution.py:158
  10.2 125.5 %copy-start.45 = (f32[512]{0:T(512)}, f32[512]{0:T(512)S(1)}, u32[]{:S(2)}) copy-start(f32[512]{0:T(512)S(1)} %convert_element_type.134) | copy-start | bytes 6148
  10.9 126.7 %copy-start.42 = (f32[512]{0:T(512)}, f32[512]{0:T(512)S(1)}, u32[]{:S(2)}) copy-start(f32[512]{0:T(512)S(1)} %convert_element_type.138) | copy-start | bytes 6148
  11.6 124.1 %copy-start.52 = (f32[512]{0:T(512)}, f32[512]{0:T(512)S(1)}, u32[]{:S(2)}) copy-start(f32[512]{0:T(512)S(1)} %convert_element_type.135) | copy-start | bytes 6148
  12.3 125.3 %copy-start.50 = (f32[512]{0:T(512)}, f32[512]{0:T(512)S(1)}, u32[]{:S(2)}) copy-start(f32[512]{0:T(512)S(1)} %convert_element_type.139) | copy-start | bytes 6148
  28.7 45.4 %copy-start.47 = (s32[128,60]{0,1:T(8,128)S(1)}, s32[128,60]{0,1:T(8,128)}, u32[]{:S(2)}) copy-start(s32[128,60]{0,1:T(8,128)} %param.28) | copy-start | bytes 92164
  28.7 45.5 %copy-start.77 = (s32[128]{0:T(128)S(1)}, s32[128]{0:T(128)}, u32[]{:S(2)}) copy-start(s32[128]{0:T(128)} %param.31) | copy-start | bytes 1540
  28.7 45.5 %copy-start.78 = (s32[128]{0:T(128)S(1)}, s32[128]{0:T(128)}, u32[]{:S(2)}) copy-start(s32[128]{0:T(128)} %param.30) | copy-start | bytes 1540
  28.8 45.8 %copy-start.14 = (bf16[1,128,512]{2,1,0:T(8,128)(2,1)S(1)}, bf16[1,128,512]{2,1,0:T(8,128)(2,1)}, u32[]{:S(2)}) copy-start(bf16[1,128,512]{2,1,0:T(8,128)(2,1)} %param.23) | copy-start | bytes 393220
  74.5 55.7 %copy-start.48 = (f32[128,60]{0,1:T(8,128)}, f32[128,60]{0,1:T(8,128)S(1)}, u32[]{:S(2)}) copy-start(f32[128,60]{0,1:T(8,128)S(1)} %copy.62) | copy-start | bytes 92164
  74.6 60.2 %copy-start.73 = (f32[128]{0:T(128)}, f32[128]{0:T(128)S(1)}, u32[]{:S(2)}) copy-start(f32[128]{0:T(128)S(1)} %broadcast_maximum_fusion) | copy-start | bytes 1540
  137.3 103.0 %copy-start.7 = (f32[128,512]{1,0:T(8,128)}, f32[128,512]{1,0:T(8,128)S(1)}, u32[]{:S(2)}) copy-start(f32[128,512]{1,0:T(8,128)S(1)} %get-tuple-element.70) | copy-start | bytes 786436
  137.4 29.6 %copy-start.54 = (f32[128]{0:T(128)}, f32[128]{0:T(128)S(1)}, u32[]{:S(2)}) copy-start(f32[128]{0:T(128)S(1)} %broadcast_multiply_fusion.1) | copy-start | bytes 1540
  137.6 29.4 %copy-start.81 = (f32[128]{0:T(128)}, f32[128]{0:T(128)S(1)}, u32[]{:S(2)}) copy-start(f32[128]{0:T(128)S(1)} %multiply_reduce_fusion.6) | copy-start | bytes 1540
  137.6 29.4 %copy-start.61 = (f32[128]{0:T(128)}, f32[128]{0:T(128)S(1)}, u32[]{:S(2)}) copy-start(f32[128]{0:T(128)S(1)} %fusion.143) | copy-start | bytes 1540
  138.4 100.2 %reduce-scatter.7.cloned.1.call-start = ((), (), s32[]{:S(2)}) async-start(), calls=%async_computation.5 | async-start | bytes 589824
  138.5 50.0 %copy-start.59 = (f32[192]{0:T(256)}, f32[192]{0:T(256)S(1)}, u32[]{:S(2)}) copy-start(f32[192]{0:T(256)S(1)} %convert_element_type.148) | copy-start | bytes 2308
  138.6 65.5 %copy-start.71 = (s32[384]{0:T(512)}, s32[384]{0:T(512)S(1)}, u32[]{:S(2)}) copy-start(s32[384]{0:T(512)S(1)} %pad_add_fusion.1) | copy-start | bytes 4612
  207.8 128.9 %reduce-scatter.5.cloned.1.call-start = ((), (), s32[]{:S(2)}) async-start(), calls=%async_computation.3 | async-start | bytes 1179648 | tf_op jit(solution)/shard_map/reduce_scatter | solution.py:224
  209.9 28.7 %copy-start.43 = (f32[512]{0:T(512)S(1)}, f32[512]{0:T(512)}, u32[]{:S(2)}) copy-start(f32[512]{0:T(512)} %copy-done.42) | copy-start | bytes 6148
  209.9 28.7 %copy-start.55 = (f32[128]{0:T(128)S(1)}, f32[128]{0:T(128)}, u32[]{:S(2)}) copy-start(f32[128]{0:T(128)} %copy-done.54) | copy-start | bytes 1540
  209.9 28.7 %copy-start.62 = (f32[128]{0:T(128)S(1)}, f32[128]{0:T(128)}, u32[]{:S(2)}) copy-start(f32[128]{0:T(128)} %copy-done.61) | copy-start | bytes 1540
  209.9 30.4 %copy-start.82 = (f32[128]{0:T(128)S(1)}, f32[128]{0:T(128)}, u32[]{:S(2)}) copy-start(f32[128]{0:T(128)} %copy-done.81) | copy-start | bytes 1540
  216.2 28.8 %copy-start.80 = (f32[128]{0:T(128)S(1)}, f32[128]{0:T(128)}, u32[]{:S(2)}) copy-start(f32[128]{0:T(128)} %copy-done.79) | copy-start | bytes 1540
  306.2 323.7 %all-reduce.7.cloned.1.call-start = ((), (), s32[]{:S(2)}) async-start(), calls=%async_computation.6 | async-start | bytes 28704768 | tf_op jit(solution)/shard_map/psum | solution.py:239
  307.8 30.1 %copy-start.31 = (f32[192,512]{1,0:T(8,128)S(1)}, f32[192,512]{1,0:T(8,128)}, u32[]{:S(2)}) copy-start(f32[192,512]{1,0:T(8,128)} %fusion.68) | copy-start | bytes 1179652
  339.7 569.6 %all-reduce.9.cloned.1.call-start = ((), (), s32[]{:S(2)}) async-start(), calls=%async_computation.7 | async-start | bytes 28704768 | tf_op jit(solution)/shard_map/psum | solution.py:238
  630.0 48.7 %copy-start.17 = (bf16[1216,512]{1,0:T(8,128)(2,1)S(1)}, bf16[1216,512]{1,0:T(8,128)(2,1)}, u32[]{:S(2)}) copy-start(bf16[1216,512]{1,0:T(8,128)(2,1)} %param.32) | copy-start | bytes 3735556
  630.0 48.7 %copy-start.21 = (f32[128,512]{1,0:T(8,128)S(1)}, f32[128,512]{1,0:T(8,128)}, u32[]{:S(2)}) copy-start(f32[128,512]{1,0:T(8,128)} %copy-done.20) | copy-start | bytes 786436
  630.0 48.7 %copy-start.76 = (f32[128]{0:T(128)S(1)}, f32[128]{0:T(128)}, u32[]{:S(2)}) copy-start(f32[128]{0:T(128)} %copy-done.75) | copy-start | bytes 1540
  (71 other events, 598.1 us)
Sparse Core Ops, SparseCore 0:
  9.6 24.7 all-gather.6
  138.5 20.3 all-gather.4
  207.9 30.6 reduce-scatter.6
  306.3 30.3 reduce-scatter.4
  341.0 288.8 all-reduce.6
  635.1 274.1 all-reduce.8
